TPU v7x, 256 devices: a whole 4x4x8 slice. The times are simulated.
256 devices in a mesh: seq: 32 (over x, y, z_lo), head: 8 (over z_hi, core).
Axes of the slice: x: 4, y: 4, z: 8 (z_hi: 4, z_lo: 2; z = z_hi * 2 + z_lo), core: 2. Of those that a mesh axis runs over, the one named last changes fastest.
Arguments:
- queries: bfloat16 [36864, 5120], P(('seq', 'head')), may hold values from -120 to 120
- key_vectors: bfloat16 [36864, 5120], P(('seq', 'head')), may hold values from -20 to 20
- value_vectors: bfloat16 [36864, 5120], P(('seq', 'head')), may hold values from -6 to 6
- reach_time: int32 [96], P('seq'), may hold values from 0 to 1
- reach_width: int32 [96], P('seq'), may hold values from 0 to 2
- keep_mask: int32 [36864, 40], P('seq', 'head'), may hold values 0 or 1
Outputs:
- attended: bfloat16 [36864, 5120], P(('seq', 'head'))
All inputs are finite; a program needn't handle non-finite values. No bound on the sum of `keep_mask` on one device may be relied on, other than what follows from the above.
Results may differ from a plain program's by a relative error of at most 0.0046.
Values may be sent and summed in bfloat16 or wider, within the bound.
A program may use at most 128 MiB of HBM per device.

v0:
```python
import math

import jax
import jax.numpy as jnp
from jax import lax
from jax.sharding import PartitionSpec as P


def extended(cells, sides, width):
    for axis, dim in sides:
        count = lax.axis_size(axis)
        ends = count - 1
        head = lax.slice_in_dim(cells, 0, width, axis=dim)
        tail = lax.slice_in_dim(cells, cells.shape[dim] - width, cells.shape[dim], axis=dim)
        cells = jnp.concatenate(
            [
                lax.ppermute(tail, axis, [(i, (i + 1) % count) for i in range(ends)]),
                cells,
                lax.ppermute(head, axis, [((i + 1) % count, i) for i in range(ends)]),
            ],
            axis=dim,
        )
    return cells


def tile_mask(reach_t, reach_w, slab_index, slab_count):
    tile_count = reach_t.shape[0]
    places = jnp.arange(tile_count, dtype=jnp.int32)
    columns = jnp.arange(3 * tile_count, dtype=jnp.int32)
    offsets = columns // tile_count - 1
    key_place = columns % tile_count
    inside = (slab_index + offsets >= 0) & (slab_index + offsets < slab_count)
    near_time = jnp.abs(offsets)[None, :] <= reach_t[:, None]
    near_width = jnp.abs(key_place[None, :] - places[:, None]) <= reach_w[:, None]
    return near_time & near_width & inside[None, :]


def head_terms(query_head, key_head, value_head, allowed):
    tile_count = allowed.shape[0]
    slab_rows = query_head.shape[0]
    tile_rows = slab_rows // tile_count
    scores = jnp.einsum("qd,kd->qk", query_head, key_head, preferred_element_type=jnp.float32) * (
        1.0 / math.sqrt(query_head.shape[1])
    )
    scores = scores.reshape(tile_count, tile_rows, 3 * tile_count, tile_rows)
    mask_full = allowed[:, None, :, None]
    scores = jnp.where(mask_full, scores, -1e30)
    highest = jnp.max(scores, axis=(2, 3), keepdims=True)
    weights = jnp.where(mask_full, jnp.exp(scores - highest), 0.0)
    totals = jnp.sum(weights, axis=(2, 3)).reshape(slab_rows)
    rounded = weights.reshape(slab_rows, 3 * slab_rows).astype(jnp.bfloat16)
    summed = jnp.dot(rounded, value_head, preferred_element_type=jnp.float32)
    return (summed, totals)


def attend_group(query_parts, wide_pairs, reach_time, reach_width):
    allowed = tile_mask(reach_time, reach_width, lax.axis_index("seq"), lax.axis_size("seq"))
    query_heads = jnp.moveaxis(query_parts[:, 0], 1, 0)
    key_heads = jnp.moveaxis(wide_pairs[0, :, 0], 1, 0)
    value_heads = jnp.moveaxis(wide_pairs[1, :, 0], 1, 0)

    def per_head(triple):
        return head_terms(triple[0], triple[1], triple[2], allowed)

    summed, totals = lax.map(per_head, (query_heads, key_heads, value_heads))
    return (jnp.moveaxis(summed, 0, 1)[:, None], jnp.moveaxis(totals, 0, 1)[:, None])


def on_device(queries, key_vectors, value_vectors, reach_time, reach_width, keep_mask):
    groups = lax.axis_size("head")
    local_rows = queries.shape[0]
    group_heads = keep_mask.shape[1]
    head_size = queries.shape[1] // (group_heads * groups)
    split_shape = (local_rows, groups, group_heads, head_size)
    query_split = queries.reshape(split_shape)
    key_split = key_vectors.reshape(split_shape)
    value_split = value_vectors.reshape(split_shape)
    query_parts, key_parts, value_parts = (
        lax.all_to_all(query_split, "head", split_axis=1, concat_axis=0, tiled=True),
        lax.all_to_all(key_split, "head", split_axis=1, concat_axis=0, tiled=True),
        lax.all_to_all(value_split, "head", split_axis=1, concat_axis=0, tiled=True),
    )
    paired = jnp.stack([key_parts, value_parts])
    wide_pairs = extended(paired, (("seq", 1),), paired.shape[1])
    summed, totals = attend_group(query_parts, wide_pairs, reach_time, reach_width)
    factor = keep_mask.astype(jnp.float32)[:, None, :, None] * (10.0 / 9.0)
    output = (summed * factor / totals[..., None]).astype(jnp.bfloat16)
    restored = lax.all_to_all(output, "head", split_axis=0, concat_axis=1, tiled=True)
    return restored.reshape(local_rows, queries.shape[1])


def solution(mesh):
    return jax.shard_map(
        on_device,
        mesh=mesh,
        in_specs=(
            P(("seq", "head"), None),
            P(("seq", "head"), None),
            P(("seq", "head"), None),
            P("seq"),
            P("seq"),
            P("seq", "head"),
        ),
        out_specs=P(("seq", "head"), None),
        check_vma=False,
    )
```

profile of v0, /device:TPU:3, one launch (start us, length us, event | category | flops | bytes accessed | tf_op | source)
XLA Modules:
  0.0 650.2 jit_solution(4315930222906517606)
XLA Ops:
  5.6 9.1 %all-to-all-start.1 = ((bf16[144,8,5,128]{3,0,2,1:T(8,128)(2,1)}), bf16[144,8,5,128]{3,0,2,1:T(8,128)(2,1)}, u32[]{:S(2)}, u32[]{:S(2)}) async-start(bf16[144,8,5,128]{3,0,2,1:T(8,128)(2,1)} %copy.24), calls=%async_computation.1 | async-start | bytes 2949120 | tf_op jit(solution)/shard_map/all_to_all | solution.py:80
  20.3 26.0 %all-to-all-done.1 = bf16[144,8,5,128]{3,0,2,1:T(8,128)(2,1)} async-done(((bf16[144,8,5,128]{3,0,2,1:T(8,128)(2,1)}), bf16[144,8,5,128]{3,0,2,1:T(8,128)(2,1)}, u32[]{:S(2)}, u32[]{:S(2)}) %all-to-all-start.1) | async-done | bytes 1474592 | tf_op jit(solution)/shard_map/all_to_all | solution.py:80
  46.4 11.1 %all-to-all-start.2 = ((bf16[144,8,5,128]{3,0,2,1:T(8,128)(2,1)}), bf16[144,8,5,128]{3,0,2,1:T(8,128)(2,1)}, u32[]{:S(2)}, u32[]{:S(2)}) async-start(bf16[144,8,5,128]{3,0,2,1:T(8,128)(2,1)} %copy.26), calls=%async_computation.2 | async-start | bytes 2949120 | tf_op jit(solution)/shard_map/all_to_all | solution.py:81
  58.9 30.4 %all-to-all-done.2 = bf16[144,8,5,128]{3,0,2,1:T(8,128)(2,1)} async-done(((bf16[144,8,5,128]{3,0,2,1:T(8,128)(2,1)}), bf16[144,8,5,128]{3,0,2,1:T(8,128)(2,1)}, u32[]{:S(2)}, u32[]{:S(2)}) %all-to-all-start.2) | async-done | bytes 1474592 | tf_op jit(solution)/shard_map/all_to_all | solution.py:81
  92.7 8.7 %collective-permute-start = (bf16[2,1152,1,5,128]{4,1,3,2,0:T(8,128)(2,1)}, bf16[2,1152,1,5,128]{4,1,3,2,0:T(8,128)(2,1)}, u32[]{:S(2)}, u32[]{:S(2)}) collective-permute-start(bf16[2,1152,1,5,128]{4,1,3,2,0:T(8,128)(2,1)} %pad_maximum_fusion.1), channel_id=1, source_target_pairs={{0,8},{8,16},{16,24},{24,32},{32,40},{40,48},{48,56},{56,64},{64,7... | collective-permute-start | bytes 8847368 | tf_op jit(solution)/shard_map/ppermute | solution.py:17
  101.4 4.3 collective-permute-start.1
  105.7 4.5 reshape.74
  114.0 6.7 %all-to-all-start = ((bf16[144,8,5,128]{3,0,2,1:T(8,128)(2,1)}), bf16[144,8,5,128]{3,0,2,1:T(8,128)(2,1)}, u32[]{:S(2)}, u32[]{:S(2)}) async-start(bf16[144,8,5,128]{3,0,2,1:T(8,128)(2,1)} %copy.22), calls=%async_computation | async-start | bytes 2949120 | tf_op jit(solution)/shard_map/all_to_all | solution.py:79
  121.9 138.2 %all-to-all-done = bf16[144,8,5,128]{3,0,2,1:T(8,128)(2,1)} async-done(((bf16[144,8,5,128]{3,0,2,1:T(8,128)(2,1)}), bf16[144,8,5,128]{3,0,2,1:T(8,128)(2,1)}, u32[]{:S(2)}, u32[]{:S(2)}) %all-to-all-start) | async-done | bytes 1474592 | tf_op jit(solution)/shard_map/all_to_all | solution.py:79
  262.7 4.2 pad_maximum_fusion
  267.0 4.2 slice_bitcast_fusion
  271.2 306.0 %while.13 = (s32[]{:T(128)}, f32[5,1152,128]{2,0,1:T(8,128)}, f32[5,1152]{1,0:T(8,128)S(1)}, bf16[5,1152,128]{2,1,0:T(8,128)(2,1)}, bf16[5,3456,128]{2,1,0:T(8,1...) while((s32[]{:T(128)}, f32[5,1152,128]{2,0,1:T(8,128)}, ...), condition=%wide.region_3.4_spmd.clone, body=%wide.region_0.3_spmd.clone.sunk | while | flops 2074261376 | bytes 99424064 | solution.py:65
  271.3 5.1 broadcast_in_dim.62
  276.4 4.5 copy.39
  280.9 4.2 copy.40
  285.1 11.5 %fusion.33 = (f32[1152]{0:T(1024)S(1)}, f32[1152,3456]{1,0:T(8,128)}) fusion(pred[1152,3456]{1,0:T(32,128)(4,1)S(1)} %copy.40, bf16[5,3456,128]{2,1,0:T(8,128)(2,1)} %get-tuple-element.203, s32[]{:T(128)} %get-tuple-element.186, bf16[5,1152,128]{2,1,0:T(8,128)(2,1)} %get-tuple-element.202), kind=kOutput, calls=%fused_computation.37.clone.1 | convolution fusion | flops 1031158656 | bytes 21091840 | tf_op jit(solution)/shard_map/while/body/eval_jaxpr/qd,kd->qk/dot_general | solution.py:42
  296.6 10.5 %fusion.35 = f32[1152]{0:T(1024)S(1)} fusion(pred[1152,3456]{1,0:T(32,128)(4,1)} %copy-done, f32[1152,3456]{1,0:T(8,128)} %get-tuple-element.171, f32[1152]{0:T(1024)S(1)} %get-tuple-element.172), kind=kLoop, calls=%fused_computation.4.clone.1 | loop fusion | flops 11942784 | bytes 19915776 | tf_op jit(solution)/shard_map/while/body/eval_jaxpr/reduce_sum | solution.py:50
  307.2 8.7 %fusion.34 = f32[1152,128]{1,0:T(8,128)S(1)} fusion(pred[1152,3456]{1,0:T(32,128)(4,1)} %copy-done, f32[1152,3456]{1,0:T(8,128)} %get-tuple-element.171, f32[1152]{0:T(1024)S(1)} %get-tuple-element.172, bf16[5,3456,128]{2,1,0:T(8,128)(2,1)} %get-tuple-element.204, s32[]{:T(128)} %get-tuple-element.186), kind=kOutput, calls=%fused_computation.6.clone.1 | convolution fusion | flops 1031159808 | bytes 21386240 | tf_op jit(solution)/shard_map/while/body/eval_jaxpr/dot_general | solution.py:52
  315.9 16.5 %dynamic_update_slice.12 = f32[5,1152,128]{2,0,1:T(8,128)} dynamic-update-slice(f32[5,1152,128]{2,0,1:T(8,128)} %get-tuple-element.187, f32[1,1152,128]{2,0,1:T(1,128)S(1)} %bitcast.77, s32[]{:T(128)} %get-tuple-element.186, s32[]{:T(128)} %constant.50.clone.1..sunk, s32[]{:T(128)} %constant.50.clone.1..sunk) | dynamic-update-slice | bytes 1179652 | tf_op jit(solution)/shard_map/while/body/jit(dynamic_update_index_in_dim)/dynamic_update_slice | solution.py:65
  332.5 5.1 broadcast_in_dim.62
  337.6 4.5 copy.39
  342.1 4.2 copy.40
  346.3 11.5 %fusion.33 = (f32[1152]{0:T(1024)S(1)}, f32[1152,3456]{1,0:T(8,128)}) fusion(pred[1152,3456]{1,0:T(32,128)(4,1)S(1)} %copy.40, bf16[5,3456,128]{2,1,0:T(8,128)(2,1)} %get-tuple-element.203, s32[]{:T(128)} %get-tuple-element.186, bf16[5,1152,128]{2,1,0:T(8,128)(2,1)} %get-tuple-element.202), kind=kOutput, calls=%fused_computation.37.clone.1 | convolution fusion | flops 1031158656 | bytes 21091840 | tf_op jit(solution)/shard_map/while/body/eval_jaxpr/qd,kd->qk/dot_general | solution.py:42
  357.8 10.5 %fusion.35 = f32[1152]{0:T(1024)S(1)} fusion(pred[1152,3456]{1,0:T(32,128)(4,1)} %copy-done, f32[1152,3456]{1,0:T(8,128)} %get-tuple-element.171, f32[1152]{0:T(1024)S(1)} %get-tuple-element.172), kind=kLoop, calls=%fused_computation.4.clone.1 | loop fusion | flops 11942784 | bytes 19915776 | tf_op jit(solution)/shard_map/while/body/eval_jaxpr/reduce_sum | solution.py:50
  368.4 8.7 %fusion.34 = f32[1152,128]{1,0:T(8,128)S(1)} fusion(pred[1152,3456]{1,0:T(32,128)(4,1)} %copy-done, f32[1152,3456]{1,0:T(8,128)} %get-tuple-element.171, f32[1152]{0:T(1024)S(1)} %get-tuple-element.172, bf16[5,3456,128]{2,1,0:T(8,128)(2,1)} %get-tuple-element.204, s32[]{:T(128)} %get-tuple-element.186), kind=kOutput, calls=%fused_computation.6.clone.1 | convolution fusion | flops 1031159808 | bytes 21386240 | tf_op jit(solution)/shard_map/while/body/eval_jaxpr/dot_general | solution.py:52
  377.1 16.5 %dynamic_update_slice.12 = f32[5,1152,128]{2,0,1:T(8,128)} dynamic-update-slice(f32[5,1152,128]{2,0,1:T(8,128)} %get-tuple-element.187, f32[1,1152,128]{2,0,1:T(1,128)S(1)} %bitcast.77, s32[]{:T(128)} %get-tuple-element.186, s32[]{:T(128)} %constant.50.clone.1..sunk, s32[]{:T(128)} %constant.50.clone.1..sunk) | dynamic-update-slice | bytes 1179652 | tf_op jit(solution)/shard_map/while/body/jit(dynamic_update_index_in_dim)/dynamic_update_slice | solution.py:65
  393.7 5.1 broadcast_in_dim.62
  398.8 4.5 copy.39
  403.3 4.2 copy.40
  407.5 11.5 %fusion.33 = (f32[1152]{0:T(1024)S(1)}, f32[1152,3456]{1,0:T(8,128)}) fusion(pred[1152,3456]{1,0:T(32,128)(4,1)S(1)} %copy.40, bf16[5,3456,128]{2,1,0:T(8,128)(2,1)} %get-tuple-element.203, s32[]{:T(128)} %get-tuple-element.186, bf16[5,1152,128]{2,1,0:T(8,128)(2,1)} %get-tuple-element.202), kind=kOutput, calls=%fused_computation.37.clone.1 | convolution fusion | flops 1031158656 | bytes 21091840 | tf_op jit(solution)/shard_map/while/body/eval_jaxpr/qd,kd->qk/dot_general | solution.py:42
  419.0 10.5 %fusion.35 = f32[1152]{0:T(1024)S(1)} fusion(pred[1152,3456]{1,0:T(32,128)(4,1)} %copy-done, f32[1152,3456]{1,0:T(8,128)} %get-tuple-element.171, f32[1152]{0:T(1024)S(1)} %get-tuple-element.172), kind=kLoop, calls=%fused_computation.4.clone.1 | loop fusion | flops 11942784 | bytes 19915776 | tf_op jit(solution)/shard_map/while/body/eval_jaxpr/reduce_sum | solution.py:50
  429.6 8.7 %fusion.34 = f32[1152,128]{1,0:T(8,128)S(1)} fusion(pred[1152,3456]{1,0:T(32,128)(4,1)} %copy-done, f32[1152,3456]{1,0:T(8,128)} %get-tuple-element.171, f32[1152]{0:T(1024)S(1)} %get-tuple-element.172, bf16[5,3456,128]{2,1,0:T(8,128)(2,1)} %get-tuple-element.204, s32[]{:T(128)} %get-tuple-element.186), kind=kOutput, calls=%fused_computation.6.clone.1 | convolution fusion | flops 1031159808 | bytes 21386240 | tf_op jit(solution)/shard_map/while/body/eval_jaxpr/dot_general | solution.py:52
  438.3 16.5 %dynamic_update_slice.12 = f32[5,1152,128]{2,0,1:T(8,128)} dynamic-update-slice(f32[5,1152,128]{2,0,1:T(8,128)} %get-tuple-element.187, f32[1,1152,128]{2,0,1:T(1,128)S(1)} %bitcast.77, s32[]{:T(128)} %get-tuple-element.186, s32[]{:T(128)} %constant.50.clone.1..sunk, s32[]{:T(128)} %constant.50.clone.1..sunk) | dynamic-update-slice | bytes 1179652 | tf_op jit(solution)/shard_map/while/body/jit(dynamic_update_index_in_dim)/dynamic_update_slice | solution.py:65
  454.9 5.1 broadcast_in_dim.62
  460.0 4.5 copy.39
  464.5 4.2 copy.40
  468.7 11.5 %fusion.33 = (f32[1152]{0:T(1024)S(1)}, f32[1152,3456]{1,0:T(8,128)}) fusion(pred[1152,3456]{1,0:T(32,128)(4,1)S(1)} %copy.40, bf16[5,3456,128]{2,1,0:T(8,128)(2,1)} %get-tuple-element.203, s32[]{:T(128)} %get-tuple-element.186, bf16[5,1152,128]{2,1,0:T(8,128)(2,1)} %get-tuple-element.202), kind=kOutput, calls=%fused_computation.37.clone.1 | convolution fusion | flops 1031158656 | bytes 21091840 | tf_op jit(solution)/shard_map/while/body/eval_jaxpr/qd,kd->qk/dot_general | solution.py:42
  480.2 10.5 %fusion.35 = f32[1152]{0:T(1024)S(1)} fusion(pred[1152,3456]{1,0:T(32,128)(4,1)} %copy-done, f32[1152,3456]{1,0:T(8,128)} %get-tuple-element.171, f32[1152]{0:T(1024)S(1)} %get-tuple-element.172), kind=kLoop, calls=%fused_computation.4.clone.1 | loop fusion | flops 11942784 | bytes 19915776 | tf_op jit(solution)/shard_map/while/body/eval_jaxpr/reduce_sum | solution.py:50
  490.8 8.7 %fusion.34 = f32[1152,128]{1,0:T(8,128)S(1)} fusion(pred[1152,3456]{1,0:T(32,128)(4,1)} %copy-done, f32[1152,3456]{1,0:T(8,128)} %get-tuple-element.171, f32[1152]{0:T(1024)S(1)} %get-tuple-element.172, bf16[5,3456,128]{2,1,0:T(8,128)(2,1)} %get-tuple-element.204, s32[]{:T(128)} %get-tuple-element.186), kind=kOutput, calls=%fused_computation.6.clone.1 | convolution fusion | flops 1031159808 | bytes 21386240 | tf_op jit(solution)/shard_map/while/body/eval_jaxpr/dot_general | solution.py:52
  499.5 16.5 %dynamic_update_slice.12 = f32[5,1152,128]{2,0,1:T(8,128)} dynamic-update-slice(f32[5,1152,128]{2,0,1:T(8,128)} %get-tuple-element.187, f32[1,1152,128]{2,0,1:T(1,128)S(1)} %bitcast.77, s32[]{:T(128)} %get-tuple-element.186, s32[]{:T(128)} %constant.50.clone.1..sunk, s32[]{:T(128)} %constant.50.clone.1..sunk) | dynamic-update-slice | bytes 1179652 | tf_op jit(solution)/shard_map/while/body/jit(dynamic_update_index_in_dim)/dynamic_update_slice | solution.py:65
  516.1 5.1 broadcast_in_dim.62
  521.2 4.5 copy.39
  529.9 11.5 %fusion.33 = (f32[1152]{0:T(1024)S(1)}, f32[1152,3456]{1,0:T(8,128)}) fusion(pred[1152,3456]{1,0:T(32,128)(4,1)S(1)} %copy.40, bf16[5,3456,128]{2,1,0:T(8,128)(2,1)} %get-tuple-element.203, s32[]{:T(128)} %get-tuple-element.186, bf16[5,1152,128]{2,1,0:T(8,128)(2,1)} %get-tuple-element.202), kind=kOutput, calls=%fused_computation.37.clone.1 | convolution fusion | flops 1031158656 | bytes 21091840 | tf_op jit(solution)/shard_map/while/body/eval_jaxpr/qd,kd->qk/dot_general | solution.py:42
  541.4 10.5 %fusion.35 = f32[1152]{0:T(1024)S(1)} fusion(pred[1152,3456]{1,0:T(32,128)(4,1)} %copy-done, f32[1152,3456]{1,0:T(8,128)} %get-tuple-element.171, f32[1152]{0:T(1024)S(1)} %get-tuple-element.172), kind=kLoop, calls=%fused_computation.4.clone.1 | loop fusion | flops 11942784 | bytes 19915776 | tf_op jit(solution)/shard_map/while/body/eval_jaxpr/reduce_sum | solution.py:50
  552.0 8.7 %fusion.34 = f32[1152,128]{1,0:T(8,128)S(1)} fusion(pred[1152,3456]{1,0:T(32,128)(4,1)} %copy-done, f32[1152,3456]{1,0:T(8,128)} %get-tuple-element.171, f32[1152]{0:T(1024)S(1)} %get-tuple-element.172, bf16[5,3456,128]{2,1,0:T(8,128)(2,1)} %get-tuple-element.204, s32[]{:T(128)} %get-tuple-element.186), kind=kOutput, calls=%fused_computation.6.clone.1 | convolution fusion | flops 1031159808 | bytes 21386240 | tf_op jit(solution)/shard_map/while/body/eval_jaxpr/dot_general | solution.py:52
  560.7 16.5 %dynamic_update_slice.12 = f32[5,1152,128]{2,0,1:T(8,128)} dynamic-update-slice(f32[5,1152,128]{2,0,1:T(8,128)} %get-tuple-element.187, f32[1,1152,128]{2,0,1:T(1,128)S(1)} %bitcast.77, s32[]{:T(128)} %get-tuple-element.186, s32[]{:T(128)} %constant.50.clone.1..sunk, s32[]{:T(128)} %constant.50.clone.1..sunk) | dynamic-update-slice | bytes 1179652 | tf_op jit(solution)/shard_map/while/body/jit(dynamic_update_index_in_dim)/dynamic_update_slice | solution.py:65
  577.4 5.6 fusion.20
  583.1 63.8 %all_to_all.60 = bf16[1152,1,5,128]{3,2,1,0:T(8,128)(2,1)S(1)} all-to-all(bf16[1152,1,5,128]{3,2,1,0:T(8,128)(2,1)S(1)} %fusion.20), channel_id=1, replica_groups=mesh['seq'=32,'head'=8] {'head'}, dimensions={0} | all-to-all | bytes 2949120 | tf_op jit(solution)/shard_map/all_to_all | solution.py:88
  (52 shorter events, 32.4 us)
Async XLA Ops:
  5.6 40.7 %all-to-all-start.1 = ((bf16[144,8,5,128]{3,0,2,1:T(8,128)(2,1)}), bf16[144,8,5,128]{3,0,2,1:T(8,128)(2,1)}, u32[]{:S(2)}, u32[]{:S(2)}) async-start(bf16[144,8,5,128]{3,0,2,1:T(8,128)(2,1)} %copy.24), calls=%async_computation.1 | async-start | bytes 2949120 | tf_op jit(solution)/shard_map/all_to_all | solution.py:80
  46.4 43.0 %all-to-all-start.2 = ((bf16[144,8,5,128]{3,0,2,1:T(8,128)(2,1)}), bf16[144,8,5,128]{3,0,2,1:T(8,128)(2,1)}, u32[]{:S(2)}, u32[]{:S(2)}) async-start(bf16[144,8,5,128]{3,0,2,1:T(8,128)(2,1)} %copy.26), calls=%async_computation.2 | async-start | bytes 2949120 | tf_op jit(solution)/shard_map/all_to_all | solution.py:81
  92.7 28.1 %copy-start.1 = (s32[1152,5]{0,1:T(8,128)S(1)}, s32[1152,5]{0,1:T(8,128)}, u32[]{:S(2)}) copy-start(s32[1152,5]{0,1:T(8,128)} %param.13) | copy-start | bytes 69124
  92.7 170.0 %collective-permute-start = (bf16[2,1152,1,5,128]{4,1,3,2,0:T(8,128)(2,1)}, bf16[2,1152,1,5,128]{4,1,3,2,0:T(8,128)(2,1)}, u32[]{:S(2)}, u32[]{:S(2)}) collective-permute-start(bf16[2,1152,1,5,128]{4,1,3,2,0:T(8,128)(2,1)} %pad_maximum_fusion.1), channel_id=1, source_target_pairs={{0,8},{8,16},{16,24},{24,32},{32,40},{40,48},{48,56},{56,64},{64,7... | collective-permute-start | bytes 8847368 | tf_op jit(solution)/shard_map/ppermute | solution.py:17
  101.4 161.3 %collective-permute-start.1 = (bf16[2,1152,1,5,128]{4,1,3,2,0:T(8,128)(2,1)}, bf16[2,1152,1,5,128]{4,1,3,2,0:T(8,128)(2,1)}, u32[]{:S(2)}, u32[]{:S(2)}) collective-permute-start(bf16[2,1152,1,5,128]{4,1,3,2,0:T(8,128)(2,1)} %pad_maximum_fusion.1), channel_id=1, source_target_pairs={{8,0},{16,8},{24,16},{32,24},{40,32},{48,40},{56,48},{64,56},{72,6... | collective-permute-start | bytes 8847368 | tf_op jit(solution)/shard_map/ppermute | solution.py:19
  114.0 146.0 %all-to-all-start = ((bf16[144,8,5,128]{3,0,2,1:T(8,128)(2,1)}), bf16[144,8,5,128]{3,0,2,1:T(8,128)(2,1)}, u32[]{:S(2)}, u32[]{:S(2)}) async-start(bf16[144,8,5,128]{3,0,2,1:T(8,128)(2,1)} %copy.22), calls=%async_computation | async-start | bytes 2949120 | tf_op jit(solution)/shard_map/all_to_all | solution.py:79
  266.9 4.2 copy-start.2
  266.9 4.2 copy-start.3
  285.1 11.5 %copy-start = (pred[1152,3456]{1,0:T(32,128)(4,1)}, pred[1152,3456]{1,0:T(32,128)(4,1)S(1)}, u32[]{:S(2)}) copy-start(pred[1152,3456]{1,0:T(32,128)(4,1)S(1)} %copy.40) | copy-start | bytes 11943940 | tf_op jit(solution)/shard_map/while
  346.3 11.5 %copy-start = (pred[1152,3456]{1,0:T(32,128)(4,1)}, pred[1152,3456]{1,0:T(32,128)(4,1)S(1)}, u32[]{:S(2)}) copy-start(pred[1152,3456]{1,0:T(32,128)(4,1)S(1)} %copy.40) | copy-start | bytes 11943940 | tf_op jit(solution)/shard_map/while
  407.5 11.5 %copy-start = (pred[1152,3456]{1,0:T(32,128)(4,1)}, pred[1152,3456]{1,0:T(32,128)(4,1)S(1)}, u32[]{:S(2)}) copy-start(pred[1152,3456]{1,0:T(32,128)(4,1)S(1)} %copy.40) | copy-start | bytes 11943940 | tf_op jit(solution)/shard_map/while
  468.7 11.5 %copy-start = (pred[1152,3456]{1,0:T(32,128)(4,1)}, pred[1152,3456]{1,0:T(32,128)(4,1)S(1)}, u32[]{:S(2)}) copy-start(pred[1152,3456]{1,0:T(32,128)(4,1)S(1)} %copy.40) | copy-start | bytes 11943940 | tf_op jit(solution)/shard_map/while
  529.9 11.5 %copy-start = (pred[1152,3456]{1,0:T(32,128)(4,1)}, pred[1152,3456]{1,0:T(32,128)(4,1)S(1)}, u32[]{:S(2)}) copy-start(pred[1152,3456]{1,0:T(32,128)(4,1)S(1)} %copy.40) | copy-start | bytes 11943940 | tf_op jit(solution)/shard_map/while
where the time goes:
time: 653 us; the launch traced here: 650 us
  waiting for transfers between devices  195 us (30%)
  local copies, waits for them, and re-layouts  186 us (28%)
  matrix products  101 us (15%)
  other arithmetic  64.5 us (10%)
  blocking collectives  63.8 us (10%)
  starting transfers between devices  40 us (6%)
    all_to_all x1, waiting for transfers between devices, on_device(): lax.all_to_all(query_split, 'head', split_axis=1, concat_axis=0, tiled=True)  138 us
    dynamic_update_slice x10, local copies, waits for them, and re-layouts, attend_group(): summed, totals = lax.map(per_head, (query_heads, key_heads, value_heads))  83.2 us
    all_to_all x1, blocking collectives, on_device(): lax.all_to_all(output, 'head', split_axis=0, concat_axis=1, tiled=True)  63.8 us
    dot_general x5, matrix products, head_terms(): jnp.einsum('qd,kd->qk', query_head, key_head, preferred_element_type=jnp....  57.3 us
    reduce_sum x5, other arithmetic, head_terms(): totals = jnp.sum(weights, axis=(2, 3)).reshape(slab_rows)  52.3 us
    broadcast_in_dim x10, local copies, waits for them, and re-layouts, head_terms(): weights = jnp.where(mask_full, jnp.exp(scores - highest), 0.0)  46.6 us
    dot_general x5, matrix products, head_terms(): summed = jnp.dot(rounded, value_head, preferred_element_type=jnp.float32)  43.3 us
    all_to_all x1, waiting for transfers between devices, on_device(): lax.all_to_all(value_split, 'head', split_axis=1, concat_axis=0, tiled=True)  30.4 us
  transfers between devices with their start and end apart: 5, of which 3 were waited for; matrix products, arithmetic and copies ran while one was open for 3% of the time, Pallas kernels for 0%

commit v1 on v0

v1 whole, which is shorter than its diff:
```python
import functools
import math

import jax
import jax.numpy as jnp
from jax import lax
from jax.experimental import pallas as pl
from jax.experimental.pallas import tpu as pltpu
from jax.sharding import PartitionSpec as P

MESH = pl.DeviceIdType.MESH
PLACES = 3
TILES = 3 * PLACES
PENALTY = 1e30


def kernel(
    group_heads, seq_count, head_count, compute,
    aux_ref, q_ref, k_ref, v_ref, o_ref,
    q_buf, k_buf, v_buf, o_buf, s_buf, p_buf, aux_buf,
    send_sem, near_sem, recv_sem, halo_send, halo_recv,
    out_send, out_near, out_recv, aux_send, aux_recv,
):
    rows, size = q_ref.shape[0], q_buf.shape[2]
    slab = q_buf.shape[1]
    tile = slab // PLACES
    columns = head_count
    scale = math.log2(math.e) / math.sqrt(size)

    seq, head = lax.axis_index("seq"), lax.axis_index("head")
    pair, low = seq // 2, seq % 2
    high, core = head // 2, head % 2
    here = high * 2 + low
    mine = pair * 2 + core
    is_self = low == core

    def at(z, of_core):
        return (pair * 2 + z % 2, (z // 2) * 2 + of_core)

    def beside(step):
        other = (mine + step + seq_count) % seq_count
        return ((other // 2) * 2 + low, high * 2 + other % 2)

    outside = beside(2 * core - 1)

    barrier = pltpu.get_barrier_semaphore()
    pl.semaphore_signal(barrier, inc=1, device_id=at(here, 1 - core), device_id_type=MESH)
    pl.semaphore_signal(barrier, inc=1, device_id=outside, device_id_type=MESH)

    def greet(step, carry):
        z = (here + step) % columns
        for of_core in range(2):
            pl.semaphore_signal(barrier, inc=1, device_id=at(z, of_core), device_id_type=MESH)
        return carry

    lax.fori_loop(1, columns, greet, 0)
    pl.semaphore_wait(barrier, 2 * columns)

    def aux_remote():
        return pltpu.make_async_remote_copy(
            src_ref=aux_ref, dst_ref=aux_buf, send_sem=aux_send, recv_sem=aux_recv,
            device_id=(pair * 2 + core, high * 2 + low), device_id_type=MESH,
        )

    @pl.when(is_self)
    def _():
        pltpu.make_async_copy(aux_ref, aux_buf, aux_recv).start()

    @pl.when(jnp.logical_not(is_self))
    def _():
        aux_remote().start()

    streams = ((k_ref, k_buf, 1), (v_ref, v_buf, 1), (q_ref, q_buf, 0))

    def landing(buf, offset, h):
        return buf.at[h, pl.ds(offset * slab, slab), :]

    def source(ref, z, h):
        return ref.at[:, pl.ds(pl.multiple_of((z * group_heads + h) * size, size), size)]

    def target(buf, offset, h):
        return buf.at[h, pl.ds(pl.multiple_of(offset * slab + head * rows, 16), rows), :]

    def send_head(h, carry):
        for t, (ref, buf, offset) in enumerate(streams):
            def send_to(step, inner, t=t, ref=ref, buf=buf, offset=offset):
                half = (step + 1) // 2
                z = (here + jnp.where(step % 2 == 1, half, columns - half)) % columns
                pltpu.make_async_remote_copy(
                    src_ref=source(ref, z, h), dst_ref=target(buf, offset, h),
                    send_sem=send_sem.at[t], recv_sem=recv_sem.at[t, h],
                    device_id=at(z, low), device_id_type=MESH,
                ).start()
                return inner

            lax.fori_loop(1, columns, send_to, 0)

            @pl.when(is_self)
            def _(t=t, ref=ref, buf=buf, offset=offset):
                pltpu.make_async_copy(source(ref, here, h), target(buf, offset, h), recv_sem.at[t, h]).start()

            @pl.when(jnp.logical_not(is_self))
            def _(t=t, ref=ref, buf=buf, offset=offset):
                pltpu.make_async_remote_copy(
                    src_ref=source(ref, here, h), dst_ref=target(buf, offset, h),
                    send_sem=near_sem.at[t], recv_sem=recv_sem.at[t, h],
                    device_id=at(here, low), device_id_type=MESH,
                ).start()
        return carry

    lax.fori_loop(0, group_heads, send_head, 0)

    def wait_for(ref, sem):
        pltpu.make_async_copy(ref, ref, sem).wait()

    def halo(t, side, h):
        buf = (k_buf, v_buf)[t]
        step = (-1, 1)[side]
        return pltpu.make_async_remote_copy(
            src_ref=landing(buf, 1, h), dst_ref=landing(buf, 1 - step, h),
            send_sem=halo_send.at[t, side, h], recv_sem=halo_recv.at[t, side, h],
            device_id=beside(step), device_id_type=MESH,
        )

    def take_head(h):
        for t, buf in enumerate((k_buf, v_buf)):
            wait_for(landing(buf, 1, h), recv_sem.at[t, h])
            for side in range(2):
                halo(t, side, h).start()

    def out_target(h):
        return o_ref.at[:, pl.ds(pl.multiple_of((here * group_heads + h) * size, size), size)]

    def send_out(h, block):
        src = o_buf.at[h, pl.ds(block * rows, rows), :]
        away = jnp.logical_or(core * columns + block != low * columns + head, False)

        @pl.when(jnp.logical_not(away))
        def _():
            pltpu.make_async_copy(src, out_target(h), out_recv).start()

        @pl.when(jnp.logical_and(away, block // 2 == high))
        def _():
            pltpu.make_async_remote_copy(
                src_ref=src, dst_ref=out_target(h), send_sem=out_near, recv_sem=out_recv,
                device_id=(pair * 2 + core, block), device_id_type=MESH,
            ).start()

        @pl.when(jnp.logical_and(away, block // 2 != high))
        def _():
            pltpu.make_async_remote_copy(
                src_ref=src, dst_ref=out_target(h), send_sem=out_send, recv_sem=out_recv,
                device_id=(pair * 2 + core, block), device_id_type=MESH,
            ).start()

    def attend(h, i):
        q = q_buf[h, i * tile:(i + 1) * tile, :]
        highest = jnp.full((tile, 128), -PENALTY, jnp.float32)
        for j in range(TILES):
            s = lax.dot_general(
                q, k_buf[h, j * tile:(j + 1) * tile, :], (((1,), (1,)), ((), ())),
                preferred_element_type=jnp.float32,
            )
            s_buf[:, j * tile:(j + 1) * tile] = s
            top = s[:, :128]
            for b in range(1, tile // 128):
                top = jnp.maximum(top, s[:, b * 128:(b + 1) * 128])
            highest = jnp.maximum(highest, top - aux_buf[5 + i:6 + i, j * 128:(j + 1) * 128])
        highest = jnp.max(highest, axis=1, keepdims=True) * scale
        total = jnp.zeros((tile, 128), jnp.float32)
        for j in range(TILES):
            level = highest + aux_buf[5 + i:6 + i, j * 128:(j + 1) * 128]
            for b in range(j * tile // 128, (j + 1) * tile // 128):
                w = jnp.exp2(s_buf[:, b * 128:(b + 1) * 128] * scale - level)
                total = total + w
                p_buf[:, b * 128:(b + 1) * 128] = w.astype(jnp.bfloat16)
        summed = jnp.dot(p_buf[...], v_buf[h], preferred_element_type=jnp.float32)
        total = jnp.sum(total, axis=1, keepdims=True)
        return summed, total

    def work_head(h):
        for t, buf in enumerate((k_buf, v_buf)):
            for side in range(2):
                halo(t, side, h).wait_recv()
        wait_for(landing(q_buf, 0, h), recv_sem.at[2, h])
        done = 0
        for i in range(PLACES):
            if compute:
                summed, total = attend(h, i)
                keep = aux_buf[pl.ds(h, 1), i * tile:(i + 1) * tile]
                keep = jnp.transpose(jnp.broadcast_to(keep, (8, tile)))[:, :1]
                o_buf[h, i * tile:(i + 1) * tile, :] = (summed * (keep / total)).astype(jnp.bfloat16)
            else:
                o_buf[h, i * tile:(i + 1) * tile, :] = q_buf[h, i * tile:(i + 1) * tile, :]
            ready = (i + 1) * tile // rows
            for block in range(done, ready):
                send_out(h, block)
            done = ready

    take_head(0)
    wait_for(aux_buf, aux_recv)

    def step(h, carry):
        take_head(h)
        work_head(h - 1)
        return carry

    lax.fori_loop(1, group_heads, step, 0)
    work_head(group_heads - 1)

    wait_for(o_ref, out_recv)
    far = (columns - 1) * group_heads * size
    near = group_heads * size
    for t, (ref, _, _) in enumerate(streams):
        wait_for(ref.at[:, :far], send_sem.at[t])

    @pl.when(jnp.logical_not(is_self))
    def _():
        aux_remote().wait_send()
        for t, (ref, _, _) in enumerate(streams):
            wait_for(ref.at[:, :near], near_sem.at[t])

    def settle(h, carry):
        for t in range(2):
            for side in range(2):
                halo(t, side, h).wait_send()
        return carry

    lax.fori_loop(0, group_heads, settle, 0)
    away_rows = (columns - 2) * rows
    wait_for(o_buf.at[:, pl.ds(0, away_rows), :], out_send)

    @pl.when(is_self)
    def _():
        wait_for(o_buf.at[:, pl.ds(0, rows), :], out_near)

    @pl.when(jnp.logical_not(is_self))
    def _():
        wait_for(o_buf.at[:, pl.ds(0, 2 * rows), :], out_near)


def tile_penalties(reach_t, reach_w, slab_index, slab_count):
    tile_count = reach_t.shape[0]
    places = jnp.arange(tile_count, dtype=jnp.int32)
    columns = jnp.arange(3 * tile_count, dtype=jnp.int32)
    offsets = columns // tile_count - 1
    key_place = columns % tile_count
    inside = (slab_index + offsets >= 0) & (slab_index + offsets < slab_count)
    near_time = jnp.abs(offsets)[None, :] <= reach_t[:, None]
    near_width = jnp.abs(key_place[None, :] - places[:, None]) <= reach_w[:, None]
    return jnp.where(near_time & near_width & inside[None, :], 0.0, PENALTY).astype(jnp.float32)


def on_device(compute, queries, key_vectors, value_vectors, reach_time, reach_width, keep_mask):
    seq_count, head_count = lax.axis_size("seq"), lax.axis_size("head")
    rows, width = queries.shape
    slab, group_heads = keep_mask.shape
    size = width // (group_heads * head_count)
    tile = slab // PLACES
    penalties = tile_penalties(reach_time, reach_width, lax.axis_index("seq"), seq_count)
    keep = keep_mask.astype(jnp.float32).T * (10.0 / 9.0)
    penalties = jnp.broadcast_to(penalties[:, :, None], (PLACES, TILES, 128)).reshape(PLACES, TILES * 128)
    wide = max(slab, TILES * 128)
    aux = jnp.concatenate([
        jnp.pad(keep, ((0, 0), (0, wide - slab))),
        jnp.pad(penalties, ((0, 0), (0, wide - TILES * 128))),
    ])
    hbm = pl.BlockSpec(memory_space=pl.ANY)
    vmem = pl.BlockSpec(memory_space=pltpu.VMEM)
    dma = pltpu.SemaphoreType.DMA
    bf16 = jnp.bfloat16
    return pl.pallas_call(
        functools.partial(kernel, group_heads, seq_count, head_count, compute),
        out_shape=jax.ShapeDtypeStruct((rows, width), bf16),
        in_specs=[vmem, hbm, hbm, hbm],
        out_specs=hbm,
        scratch_shapes=[
            pltpu.VMEM((group_heads, slab, size), bf16),
            pltpu.VMEM((group_heads, 3 * slab, size), bf16),
            pltpu.VMEM((group_heads, 3 * slab, size), bf16),
            pltpu.VMEM((group_heads, slab, size), bf16),
            pltpu.VMEM((tile, 3 * slab), jnp.float32),
            pltpu.VMEM((tile, 3 * slab), bf16),
            pltpu.VMEM(aux.shape, jnp.float32),
            dma((3,)), dma((3,)), dma((3, group_heads)),
            dma((2, 2, group_heads)), dma((2, 2, group_heads)),
            dma, dma, dma, dma, dma,
        ],
        compiler_params=pltpu.CompilerParams(
            collective_id=0, has_side_effects=True, vmem_limit_bytes=48 * 1024 * 1024
        ),
    )(aux, queries, key_vectors, value_vectors)


def solution(mesh, compute=True):
    return jax.shard_map(
        functools.partial(on_device, compute),
        mesh=mesh,
        in_specs=(
            P(("seq", "head"), None),
            P(("seq", "head"), None),
            P(("seq", "head"), None),
            P("seq"),
            P("seq"),
            P("seq", "head"),
        ),
        out_specs=P(("seq", "head"), None),
        check_vma=False,
    )
```

time: 653 us -> 145 us (0.22)
  waiting for transfers between devices: 195 us -> 0 us
  local copies, waits for them, and re-layouts: 186 us -> 5.31 us
  Pallas kernels: 0 us -> 137 us
  matrix products: 101 us -> 0 us
  blocking collectives: 63.8 us -> 0 us
  other arithmetic: 64.5 us -> 1.57 us
  starting transfers between devices: 40 us -> 0 us
    all_to_all x3 -> x0, waiting for transfers between devices: 195 us -> none  [the longest x1 138 us: on_device(): lax.all_to_all(query_split, 'head', split_axis=1, concat_axis=0, tiled=True)]
    pallas_call x0 -> x1, Pallas kernels: none -> 137 us  [on_device(): pl.pallas_call(functools.partial(kernel, group_heads, seq_count, head_cou...]
    dot_general x10 -> x0, matrix products: 101 us -> none  [the longest x5 57.3 us: head_terms(): jnp.einsum('qd,kd->qk', query_head, key_head, preferred_element_type=jnp....]
    dynamic_update_slice x10 -> x0, local copies, waits for them, and re-layouts: 83.2 us -> none  [attend_group(): summed, totals = lax.map(per_head, (query_heads, key_heads, value_heads))]
    all_to_all x1 -> x0, blocking collectives: 63.8 us -> none  [on_device(): lax.all_to_all(output, 'head', split_axis=0, concat_axis=1, tiled=True)]
    reduce_sum x5 -> x0, other arithmetic: 52.3 us -> none  [head_terms(): totals = jnp.sum(weights, axis=(2, 3)).reshape(slab_rows)]
    broadcast_in_dim x15 -> x0, local copies, waits for them, and re-layouts: 46.6 us -> none  [the longest x10 46.6 us: head_terms(): weights = jnp.where(mask_full, jnp.exp(scores - highest), 0.0)]
    all_to_all x3 -> x0, starting transfers between devices: 26.9 us -> none  [the longest x1 11.1 us: on_device(): lax.all_to_all(value_split, 'head', split_axis=1, concat_axis=0, tiled=True)]
  transfers between devices with their start and end apart: 5 -> 0, of which waited for: 3 -> 0; matrix products, arithmetic and copies ran while one was open for 3% -> 0% of each run, Pallas kernels for 0% -> 0%
where the time goes in v1:
time: 145 us; the launch traced here: 144 us
  Pallas kernels  137 us (94%)
  local copies, waits for them, and re-layouts  5.31 us (4%)
  other arithmetic  1.57 us (1%)
    pallas_call x1, Pallas kernels, on_device(): pl.pallas_call(functools.partial(kernel, group_heads, seq_count, head_cou...  137 us
    unnamed x9, local copies, waits for them, and re-layouts  5.31 us

profile of v1, /device:TPU:3, one launch (start us, length us, event | category | flops | bytes accessed | tf_op | source)
XLA Modules:
  0.0 143.7 jit_solution(15875458751683211183)
XLA Ops:
  0.0 0.7 fusion.2
  0.8 0.1 broadcast_bitcast_fusion
  0.9 0.8 multiply_bitcast_fusion
  1.7 0.0 copy-start
  1.7 1.4 copy-done
  3.0 0.0 copy-start.1
  3.0 1.4 copy-done.1
  4.4 0.0 copy-start.2
  4.4 1.4 copy-done.2
  5.8 136.8 %shard_map.64 = bf16[144,5120]{1,0:T(8,128)(2,1)S(1)} custom-call(f32[8,1152]{1,0:T(8,128)S(1)} %pad_maximum_fusion.aux_ref, bf16[144,5120]{1,0:T(8,128)(2,1)S(1)} %copy-done, bf16[144,5120]{1,0:T(8,128)(2,1)S(1)} %copy-done.1, bf16[144,5120]{1,0:T(8,128)(2,1)S(1)} %copy-done.2), custom_call_target="tpu_custom_call" | custom-call | tf_op jit(solution)/shard_map/pallas_call | solution.py:272
  142.6 1.1 copy.11
  (4 shorter events, 0.1 us)
Async XLA Ops:
  1.7 1.4 copy-start
  3.0 1.4 copy-start.1
  4.4 1.4 copy-start.2

commit v2 on v1

--- a/solution.py
+++ b/solution.py
@@ -16,10 +16,11 @@
 
 def kernel(
     group_heads, seq_count, head_count, compute,
-    aux_ref, q_ref, k_ref, v_ref, o_ref,
-    q_buf, k_buf, v_buf, o_buf, s_buf, p_buf, aux_buf,
+    keep_ref, time_ref, width_ref, q_ref, k_ref, v_ref, o_ref,
+    q_buf, k_buf, v_buf, o_buf, s_buf, p_buf, aux_ref, aux_buf,
+    keep_buf, time_buf, width_buf, src_buf,
     send_sem, near_sem, recv_sem, halo_send, halo_recv,
-    out_send, out_near, out_recv, aux_send, aux_recv,
+    out_send, out_near, out_recv, aux_send, aux_recv, small_sem, src_sem,
 ):
     rows, size = q_ref.shape[0], q_buf.shape[2]
     slab = q_buf.shape[1]
@@ -43,6 +44,19 @@
 
     outside = beside(2 * core - 1)
 
+    loads = [
+        pltpu.make_async_copy(src, src_buf.at[t], src_sem.at[t])
+        for t, src in enumerate((k_ref, v_ref, q_ref))
+    ]
+    for copy in loads:
+        copy.start()
+    smalls = [
+        pltpu.make_async_copy(src, dst, small_sem.at[n])
+        for n, (src, dst) in enumerate(((keep_ref, keep_buf), (time_ref, time_buf), (width_ref, width_buf)))
+    ]
+    for copy in smalls:
+        copy.start()
+
     barrier = pltpu.get_barrier_semaphore()
     pl.semaphore_signal(barrier, inc=1, device_id=at(here, 1 - core), device_id_type=MESH)
     pl.semaphore_signal(barrier, inc=1, device_id=outside, device_id_type=MESH)
@@ -62,15 +76,7 @@
             device_id=(pair * 2 + core, high * 2 + low), device_id_type=MESH,
         )
 
-    @pl.when(is_self)
-    def _():
-        pltpu.make_async_copy(aux_ref, aux_buf, aux_recv).start()
-
-    @pl.when(jnp.logical_not(is_self))
-    def _():
-        aux_remote().start()
-
-    streams = ((k_ref, k_buf, 1), (v_ref, v_buf, 1), (q_ref, q_buf, 0))
+    streams = ((src_buf.at[0], k_buf, 1), (src_buf.at[1], v_buf, 1), (src_buf.at[2], q_buf, 0))
 
     def landing(buf, offset, h):
         return buf.at[h, pl.ds(offset * slab, slab), :]
@@ -108,7 +114,28 @@
                 ).start()
         return carry
 
+    for copy in loads:
+        copy.wait()
     lax.fori_loop(0, group_heads, send_head, 0)
+
+    for copy in smalls:
+        copy.wait()
+    aux_ref[0:group_heads, :] = keep_buf[...].astype(jnp.float32) * (10.0 / 9.0)
+    for i in range(PLACES):
+        for j in range(TILES):
+            offset, place = j // PLACES - 1, j % PLACES
+            near = jnp.logical_and(abs(offset) <= time_buf[i], abs(place - i) <= width_buf[i])
+            inside = jnp.logical_and(seq + offset >= 0, seq + offset < seq_count)
+            penalty = jnp.where(jnp.logical_and(near, inside), 0.0, PENALTY).astype(jnp.float32)
+            aux_ref[group_heads + i:group_heads + i + 1, j * 128:(j + 1) * 128] = jnp.full((1, 128), penalty)
+
+    @pl.when(is_self)
+    def _():
+        pltpu.make_async_copy(aux_ref, aux_buf, aux_recv).start()
+
+    @pl.when(jnp.logical_not(is_self))
+    def _():
+        aux_remote().start()
 
     def wait_for(ref, sem):
         pltpu.make_async_copy(ref, ref, sem).wait()
@@ -165,11 +192,11 @@
             top = s[:, :128]
             for b in range(1, tile // 128):
                 top = jnp.maximum(top, s[:, b * 128:(b + 1) * 128])
-            highest = jnp.maximum(highest, top - aux_buf[5 + i:6 + i, j * 128:(j + 1) * 128])
+            highest = jnp.maximum(highest, top - aux_buf[group_heads + i:group_heads + i + 1, j * 128:(j + 1) * 128])
         highest = jnp.max(highest, axis=1, keepdims=True) * scale
         total = jnp.zeros((tile, 128), jnp.float32)
         for j in range(TILES):
-            level = highest + aux_buf[5 + i:6 + i, j * 128:(j + 1) * 128]
+            level = highest + aux_buf[group_heads + i:group_heads + i + 1, j * 128:(j + 1) * 128]
             for b in range(j * tile // 128, (j + 1) * tile // 128):
                 w = jnp.exp2(s_buf[:, b * 128:(b + 1) * 128] * scale - level)
                 total = total + w
@@ -239,41 +266,21 @@
         wait_for(o_buf.at[:, pl.ds(0, 2 * rows), :], out_near)
 
 
-def tile_penalties(reach_t, reach_w, slab_index, slab_count):
-    tile_count = reach_t.shape[0]
-    places = jnp.arange(tile_count, dtype=jnp.int32)
-    columns = jnp.arange(3 * tile_count, dtype=jnp.int32)
-    offsets = columns // tile_count - 1
-    key_place = columns % tile_count
-    inside = (slab_index + offsets >= 0) & (slab_index + offsets < slab_count)
-    near_time = jnp.abs(offsets)[None, :] <= reach_t[:, None]
-    near_width = jnp.abs(key_place[None, :] - places[:, None]) <= reach_w[:, None]
-    return jnp.where(near_time & near_width & inside[None, :], 0.0, PENALTY).astype(jnp.float32)
-
-
 def on_device(compute, queries, key_vectors, value_vectors, reach_time, reach_width, keep_mask):
     seq_count, head_count = lax.axis_size("seq"), lax.axis_size("head")
     rows, width = queries.shape
     slab, group_heads = keep_mask.shape
     size = width // (group_heads * head_count)
     tile = slab // PLACES
-    penalties = tile_penalties(reach_time, reach_width, lax.axis_index("seq"), seq_count)
-    keep = keep_mask.astype(jnp.float32).T * (10.0 / 9.0)
-    penalties = jnp.broadcast_to(penalties[:, :, None], (PLACES, TILES, 128)).reshape(PLACES, TILES * 128)
-    wide = max(slab, TILES * 128)
-    aux = jnp.concatenate([
-        jnp.pad(keep, ((0, 0), (0, wide - slab))),
-        jnp.pad(penalties, ((0, 0), (0, wide - TILES * 128))),
-    ])
-    hbm = pl.BlockSpec(memory_space=pl.ANY)
-    vmem = pl.BlockSpec(memory_space=pltpu.VMEM)
+    aux_shape = (group_heads + PLACES, max(slab, TILES * 128))
+    hbm = pl.BlockSpec(memory_space=pltpu.HBM)
     dma = pltpu.SemaphoreType.DMA
     bf16 = jnp.bfloat16
     return pl.pallas_call(
         functools.partial(kernel, group_heads, seq_count, head_count, compute),
         out_shape=jax.ShapeDtypeStruct((rows, width), bf16),
-        in_specs=[vmem, hbm, hbm, hbm],
-        out_specs=hbm,
+        in_specs=[hbm] * 6,
+        out_specs=pl.BlockSpec(memory_space=pltpu.VMEM),
         scratch_shapes=[
             pltpu.VMEM((group_heads, slab, size), bf16),
             pltpu.VMEM((group_heads, 3 * slab, size), bf16),
@@ -281,15 +288,20 @@
             pltpu.VMEM((group_heads, slab, size), bf16),
             pltpu.VMEM((tile, 3 * slab), jnp.float32),
             pltpu.VMEM((tile, 3 * slab), bf16),
-            pltpu.VMEM(aux.shape, jnp.float32),
+            pltpu.VMEM(aux_shape, jnp.float32),
+            pltpu.VMEM(aux_shape, jnp.float32),
+            pltpu.VMEM((group_heads, slab), jnp.int32),
+            pltpu.SMEM(reach_time.shape, jnp.int32),
+            pltpu.SMEM(reach_width.shape, jnp.int32),
+            pltpu.VMEM((3, rows, width), bf16),
             dma((3,)), dma((3,)), dma((3, group_heads)),
             dma((2, 2, group_heads)), dma((2, 2, group_heads)),
-            dma, dma, dma, dma, dma,
+            dma, dma, dma, dma, dma, dma((3,)), dma((3,)),
         ],
         compiler_params=pltpu.CompilerParams(
             collective_id=0, has_side_effects=True, vmem_limit_bytes=48 * 1024 * 1024
         ),
-    )(aux, queries, key_vectors, value_vectors)
+    )(*(pltpu.with_memory_space_constraint(x, pltpu.HBM) for x in (keep_mask.T, reach_time, reach_width, queries, key_vectors, value_vectors)))
 
 
 def solution(mesh, compute=True):

time: 145 us -> 169 us (1.17)
  Pallas kernels: 137 us -> 168 us
  local copies, waits for them, and re-layouts: 5.31 us -> 1.11 us
    pallas_call x1, Pallas kernels: 137 us -> 168 us  [on_device(): pl.pallas_call(functools.partial(kernel, group_heads, seq_count, head_cou...]
    unnamed x9 -> x1, local copies, waits for them, and re-layouts: 5.31 us -> 1.11 us
where the time goes in v2:
time: 169 us
  Pallas kernels  168 us (99%)
    pallas_call x1, Pallas kernels, on_device(): pl.pallas_call(functools.partial(kernel, group_heads, seq_count, head_cou...  168 us

profile of v2, /device:TPU:3, one launch (start us, length us, event | category | flops | bytes accessed | tf_op | source)
XLA Modules:
  0.0 168.9 jit_solution(4632085579207558119)
XLA Ops:
  0.0 167.8 %shard_map.64 = bf16[144,5120]{1,0:T(8,128)(2,1)S(1)} custom-call(s32[5,1152]{1,0:T(8,128)} %bitcast.1, s32[3]{0:T(128)} %time_ref.1, s32[3]{0:T(128)} %width_ref.1, bf16[144,5120]{1,0:T(8,128)(2,1)} %q_ref.1, bf16[144,5120]{1,0:T(8,128)(2,1)} %k_ref.1, bf16[144,5120]{1,0:T(8,128)(2,1)} %v_ref.1), custom_call_target="tpu_custom_call" | custom-call | tf_op jit(solution)/shard_map/pallas_call | solution.py:279
  167.8 1.1 copy.8

commit v3 on v2

--- a/solution.py
+++ b/solution.py
@@ -18,9 +18,9 @@
     group_heads, seq_count, head_count, compute,
     keep_ref, time_ref, width_ref, q_ref, k_ref, v_ref, o_ref,
     q_buf, k_buf, v_buf, o_buf, s_buf, p_buf, aux_ref, aux_buf,
-    keep_buf, time_buf, width_buf, src_buf,
+    keep_buf, time_buf, width_buf,
     send_sem, near_sem, recv_sem, halo_send, halo_recv,
-    out_send, out_near, out_recv, aux_send, aux_recv, small_sem, src_sem,
+    out_send, out_near, out_recv, aux_send, aux_recv, small_sem,
 ):
     rows, size = q_ref.shape[0], q_buf.shape[2]
     slab = q_buf.shape[1]
@@ -44,12 +44,6 @@
 
     outside = beside(2 * core - 1)
 
-    loads = [
-        pltpu.make_async_copy(src, src_buf.at[t], src_sem.at[t])
-        for t, src in enumerate((k_ref, v_ref, q_ref))
-    ]
-    for copy in loads:
-        copy.start()
     smalls = [
         pltpu.make_async_copy(src, dst, small_sem.at[n])
         for n, (src, dst) in enumerate(((keep_ref, keep_buf), (time_ref, time_buf), (width_ref, width_buf)))
@@ -68,6 +62,17 @@
         return carry
 
     lax.fori_loop(1, columns, greet, 0)
+    for copy in smalls:
+        copy.wait()
+    aux_ref[0:group_heads, :] = keep_buf[...].astype(jnp.float32) * (10.0 / 9.0)
+    for i in range(PLACES):
+        for j in range(TILES):
+            offset, place = j // PLACES - 1, j % PLACES
+            near = jnp.logical_and(abs(offset) <= time_buf[i], abs(place - i) <= width_buf[i])
+            inside = jnp.logical_and(seq + offset >= 0, seq + offset < seq_count)
+            penalty = jnp.where(jnp.logical_and(near, inside), 0.0, PENALTY).astype(jnp.float32)
+            aux_ref[group_heads + i:group_heads + i + 1, j * 128:(j + 1) * 128] = jnp.full((1, 128), penalty)
+
     pl.semaphore_wait(barrier, 2 * columns)
 
     def aux_remote():
@@ -76,7 +81,15 @@
             device_id=(pair * 2 + core, high * 2 + low), device_id_type=MESH,
         )
 
-    streams = ((src_buf.at[0], k_buf, 1), (src_buf.at[1], v_buf, 1), (src_buf.at[2], q_buf, 0))
+    @pl.when(is_self)
+    def _():
+        pltpu.make_async_copy(aux_ref, aux_buf, aux_recv).start()
+
+    @pl.when(jnp.logical_not(is_self))
+    def _():
+        aux_remote().start()
+
+    streams = ((k_ref, k_buf, 1), (v_ref, v_buf, 1), (q_ref, q_buf, 0))
 
     def landing(buf, offset, h):
         return buf.at[h, pl.ds(offset * slab, slab), :]
@@ -114,28 +127,7 @@
                 ).start()
         return carry
 
-    for copy in loads:
-        copy.wait()
     lax.fori_loop(0, group_heads, send_head, 0)
-
-    for copy in smalls:
-        copy.wait()
-    aux_ref[0:group_heads, :] = keep_buf[...].astype(jnp.float32) * (10.0 / 9.0)
-    for i in range(PLACES):
-        for j in range(TILES):
-            offset, place = j // PLACES - 1, j % PLACES
-            near = jnp.logical_and(abs(offset) <= time_buf[i], abs(place - i) <= width_buf[i])
-            inside = jnp.logical_and(seq + offset >= 0, seq + offset < seq_count)
-            penalty = jnp.where(jnp.logical_and(near, inside), 0.0, PENALTY).astype(jnp.float32)
-            aux_ref[group_heads + i:group_heads + i + 1, j * 128:(j + 1) * 128] = jnp.full((1, 128), penalty)
-
-    @pl.when(is_self)
-    def _():
-        pltpu.make_async_copy(aux_ref, aux_buf, aux_recv).start()
-
-    @pl.when(jnp.logical_not(is_self))
-    def _():
-        aux_remote().start()
 
     def wait_for(ref, sem):
         pltpu.make_async_copy(ref, ref, sem).wait()
@@ -293,10 +285,9 @@
             pltpu.VMEM((group_heads, slab), jnp.int32),
             pltpu.SMEM(reach_time.shape, jnp.int32),
             pltpu.SMEM(reach_width.shape, jnp.int32),
-            pltpu.VMEM((3, rows, width), bf16),
             dma((3,)), dma((3,)), dma((3, group_heads)),
             dma((2, 2, group_heads)), dma((2, 2, group_heads)),
-            dma, dma, dma, dma, dma, dma((3,)), dma((3,)),
+            dma, dma, dma, dma, dma, dma((3,)),
         ],
         compiler_params=pltpu.CompilerParams(
             collective_id=0, has_side_effects=True, vmem_limit_bytes=48 * 1024 * 1024

time: 169 us -> 139 us (0.82)
  Pallas kernels: 168 us -> 137 us
    pallas_call x1, Pallas kernels: 168 us -> 137 us  [on_device(): pl.pallas_call(functools.partial(kernel, group_heads, seq_count, head_cou...]
where the time goes in v3:
time: 139 us; the launch traced here: 138 us
  Pallas kernels  137 us (99%)
    pallas_call x1, Pallas kernels, on_device(): pl.pallas_call(functools.partial(kernel, group_heads, seq_count, head_cou...  137 us

profile of v3, /device:TPU:3, one launch (start us, length us, event | category | flops | bytes accessed | tf_op | source)
XLA Modules:
  0.0 138.1 jit_solution(15090303377447928159)
XLA Ops:
  0.0 137.0 %shard_map.64 = bf16[144,5120]{1,0:T(8,128)(2,1)S(1)} custom-call(s32[5,1152]{1,0:T(8,128)} %bitcast.1, s32[3]{0:T(128)} %time_ref.1, s32[3]{0:T(128)} %width_ref.1, bf16[144,5120]{1,0:T(8,128)(2,1)} %q_ref.1, bf16[144,5120]{1,0:T(8,128)(2,1)} %k_ref.1, bf16[144,5120]{1,0:T(8,128)(2,1)} %v_ref.1), custom_call_target="tpu_custom_call" | custom-call | tf_op jit(solution)/shard_map/pallas_call | solution.py:271
  137.0 1.1 copy.8

commit v4 on v2

--- a/solution.py
+++ b/solution.py
@@ -18,9 +18,9 @@
     group_heads, seq_count, head_count, compute,
     keep_ref, time_ref, width_ref, q_ref, k_ref, v_ref, o_ref,
     q_buf, k_buf, v_buf, o_buf, s_buf, p_buf, aux_ref, aux_buf,
-    keep_buf, time_buf, width_buf, src_buf,
+    keep_buf, time_buf, width_buf,
     send_sem, near_sem, recv_sem, halo_send, halo_recv,
-    out_send, out_near, out_recv, aux_send, aux_recv, small_sem, src_sem,
+    out_send, out_near, out_recv, aux_send, aux_recv, small_sem,
 ):
     rows, size = q_ref.shape[0], q_buf.shape[2]
     slab = q_buf.shape[1]
@@ -44,12 +44,6 @@
 
     outside = beside(2 * core - 1)
 
-    loads = [
-        pltpu.make_async_copy(src, src_buf.at[t], src_sem.at[t])
-        for t, src in enumerate((k_ref, v_ref, q_ref))
-    ]
-    for copy in loads:
-        copy.start()
     smalls = [
         pltpu.make_async_copy(src, dst, small_sem.at[n])
         for n, (src, dst) in enumerate(((keep_ref, keep_buf), (time_ref, time_buf), (width_ref, width_buf)))
@@ -76,7 +70,7 @@
             device_id=(pair * 2 + core, high * 2 + low), device_id_type=MESH,
         )
 
-    streams = ((src_buf.at[0], k_buf, 1), (src_buf.at[1], v_buf, 1), (src_buf.at[2], q_buf, 0))
+    streams = ((k_ref, k_buf, 1), (v_ref, v_buf, 1), (q_ref, q_buf, 0))
 
     def landing(buf, offset, h):
         return buf.at[h, pl.ds(offset * slab, slab), :]
@@ -87,37 +81,41 @@
     def target(buf, offset, h):
         return buf.at[h, pl.ds(pl.multiple_of(offset * slab + head * rows, 16), rows), :]
 
-    def send_head(h, carry):
-        for t, (ref, buf, offset) in enumerate(streams):
-            def send_to(step, inner, t=t, ref=ref, buf=buf, offset=offset):
-                half = (step + 1) // 2
-                z = (here + jnp.where(step % 2 == 1, half, columns - half)) % columns
-                pltpu.make_async_remote_copy(
-                    src_ref=source(ref, z, h), dst_ref=target(buf, offset, h),
-                    send_sem=send_sem.at[t], recv_sem=recv_sem.at[t, h],
-                    device_id=at(z, low), device_id_type=MESH,
-                ).start()
-                return inner
-
-            lax.fori_loop(1, columns, send_to, 0)
-
-            @pl.when(is_self)
-            def _(t=t, ref=ref, buf=buf, offset=offset):
-                pltpu.make_async_copy(source(ref, here, h), target(buf, offset, h), recv_sem.at[t, h]).start()
-
-            @pl.when(jnp.logical_not(is_self))
-            def _(t=t, ref=ref, buf=buf, offset=offset):
-                pltpu.make_async_remote_copy(
-                    src_ref=source(ref, here, h), dst_ref=target(buf, offset, h),
-                    send_sem=near_sem.at[t], recv_sem=recv_sem.at[t, h],
-                    device_id=at(here, low), device_id_type=MESH,
-                ).start()
+    def send(t, h):
+        ref, buf, offset = streams[t]
+
+        def send_to(step, carry):
+            half = (step + 1) // 2
+            z = (here + jnp.where(step % 2 == 1, half, columns - half)) % columns
+            pltpu.make_async_remote_copy(
+                src_ref=source(ref, z, h), dst_ref=target(buf, offset, h),
+                send_sem=send_sem.at[t], recv_sem=recv_sem.at[t, h],
+                device_id=at(z, low), device_id_type=MESH,
+            ).start()
+            return carry
+
+        lax.fori_loop(1, columns, send_to, 0)
+
+        @pl.when(is_self)
+        def _():
+            pltpu.make_async_copy(source(ref, here, h), target(buf, offset, h), recv_sem.at[t, h]).start()
+
+        @pl.when(jnp.logical_not(is_self))
+        def _():
+            pltpu.make_async_remote_copy(
+                src_ref=source(ref, here, h), dst_ref=target(buf, offset, h),
+                send_sem=near_sem.at[t], recv_sem=recv_sem.at[t, h],
+                device_id=at(here, low), device_id_type=MESH,
+            ).start()
+
+    def send_heads(h, carry):
+        send(0, h)
+        send(1, h)
+        send(2, h)
         return carry
 
-    for copy in loads:
-        copy.wait()
-    lax.fori_loop(0, group_heads, send_head, 0)
-
+    send(0, 0)
+    send(1, 0)
     for copy in smalls:
         copy.wait()
     aux_ref[0:group_heads, :] = keep_buf[...].astype(jnp.float32) * (10.0 / 9.0)
@@ -137,6 +135,9 @@
     def _():
         aux_remote().start()
 
+    send(2, 0)
+    lax.fori_loop(1, group_heads, send_heads, 0)
+
     def wait_for(ref, sem):
         pltpu.make_async_copy(ref, ref, sem).wait()
 
@@ -159,8 +160,8 @@
         return o_ref.at[:, pl.ds(pl.multiple_of((here * group_heads + h) * size, size), size)]
 
     def send_out(h, block):
-        src = o_buf.at[h, pl.ds(block * rows, rows), :]
-        away = jnp.logical_or(core * columns + block != low * columns + head, False)
+        src = o_buf.at[h, pl.ds(pl.multiple_of(block * rows, 16), rows), :]
+        away = core * columns + block != low * columns + head
 
         @pl.when(jnp.logical_not(away))
         def _():
@@ -205,7 +206,7 @@
         total = jnp.sum(total, axis=1, keepdims=True)
         return summed, total
 
-    def work_head(h):
+    def work_head(h, last=False):
         for t, buf in enumerate((k_buf, v_buf)):
             for side in range(2):
                 halo(t, side, h).wait_recv()
@@ -219,10 +220,17 @@
                 o_buf[h, i * tile:(i + 1) * tile, :] = (summed * (keep / total)).astype(jnp.bfloat16)
             else:
                 o_buf[h, i * tile:(i + 1) * tile, :] = q_buf[h, i * tile:(i + 1) * tile, :]
-            ready = (i + 1) * tile // rows
-            for block in range(done, ready):
-                send_out(h, block)
-            done = ready
+            if last:
+                ready = (i + 1) * tile // rows
+                for block in ((1, 0), (3, 2, 4), (5, 7, 6))[i]:
+                    send_out(h, block)
+                done = ready
+        if not last:
+            def send_rest(step, carry):
+                send_out(h, step + 1 - 2 * (step % 2))
+                return carry
+
+            lax.fori_loop(0, columns, send_rest, 0)
 
     take_head(0)
     wait_for(aux_buf, aux_recv)
@@ -233,7 +241,7 @@
         return carry
 
     lax.fori_loop(1, group_heads, step, 0)
-    work_head(group_heads - 1)
+    work_head(group_heads - 1, last=True)
 
     wait_for(o_ref, out_recv)
     far = (columns - 1) * group_heads * size
@@ -293,10 +301,9 @@
             pltpu.VMEM((group_heads, slab), jnp.int32),
             pltpu.SMEM(reach_time.shape, jnp.int32),
             pltpu.SMEM(reach_width.shape, jnp.int32),
-            pltpu.VMEM((3, rows, width), bf16),
             dma((3,)), dma((3,)), dma((3, group_heads)),
             dma((2, 2, group_heads)), dma((2, 2, group_heads)),
-            dma, dma, dma, dma, dma, dma((3,)), dma((3,)),
+            dma, dma, dma, dma, dma, dma((3,)),
         ],
         compiler_params=pltpu.CompilerParams(
             collective_id=0, has_side_effects=True, vmem_limit_bytes=48 * 1024 * 1024

time: 169 us -> 138 us (0.82)
  Pallas kernels: 168 us -> 136 us
    pallas_call x1, Pallas kernels: 168 us -> 136 us  [on_device(): pl.pallas_call(functools.partial(kernel, group_heads, seq_count, head_cou...]
where the time goes in v4:
time: 138 us; the launch traced here: 137 us
  Pallas kernels  136 us (99%)
    pallas_call x1, Pallas kernels, on_device(): pl.pallas_call(functools.partial(kernel, group_heads, seq_count, head_cou...  136 us

profile of v4, /device:TPU:3, one launch (start us, length us, event | category | flops | bytes accessed | tf_op | source)
XLA Modules:
  0.0 136.6 jit_solution(519938873900771018)
XLA Ops:
  0.0 135.5 %shard_map.64 = bf16[144,5120]{1,0:T(8,128)(2,1)S(1)} custom-call(s32[5,1152]{1,0:T(8,128)} %bitcast.1, s32[3]{0:T(128)} %time_ref.1, s32[3]{0:T(128)} %width_ref.1, bf16[144,5120]{1,0:T(8,128)(2,1)} %q_ref.1, bf16[144,5120]{1,0:T(8,128)(2,1)} %k_ref.1, bf16[144,5120]{1,0:T(8,128)(2,1)} %v_ref.1), custom_call_target="tpu_custom_call" | custom-call | tf_op jit(solution)/shard_map/pallas_call | solution.py:287
  135.5 1.1 copy.8

commit v5 on v4

--- a/solution.py
+++ b/solution.py
@@ -44,6 +44,17 @@
 
     outside = beside(2 * core - 1)
 
+    barrier = pltpu.get_barrier_semaphore()
+    pl.semaphore_signal(barrier, inc=1, device_id=at(here, 1 - core), device_id_type=MESH)
+    pl.semaphore_signal(barrier, inc=1, device_id=outside, device_id_type=MESH)
+
+    def greet(step, carry):
+        z = (here + step) % columns
+        for of_core in range(2):
+            pl.semaphore_signal(barrier, inc=1, device_id=at(z, of_core), device_id_type=MESH)
+        return carry
+
+    lax.fori_loop(1, columns, greet, 0)
     smalls = [
         pltpu.make_async_copy(src, dst, small_sem.at[n])
         for n, (src, dst) in enumerate(((keep_ref, keep_buf), (time_ref, time_buf), (width_ref, width_buf)))
@@ -51,17 +62,6 @@
     for copy in smalls:
         copy.start()
 
-    barrier = pltpu.get_barrier_semaphore()
-    pl.semaphore_signal(barrier, inc=1, device_id=at(here, 1 - core), device_id_type=MESH)
-    pl.semaphore_signal(barrier, inc=1, device_id=outside, device_id_type=MESH)
-
-    def greet(step, carry):
-        z = (here + step) % columns
-        for of_core in range(2):
-            pl.semaphore_signal(barrier, inc=1, device_id=at(z, of_core), device_id_type=MESH)
-        return carry
-
-    lax.fori_loop(1, columns, greet, 0)
     pl.semaphore_wait(barrier, 2 * columns)
 
     def aux_remote():
@@ -227,7 +227,7 @@
                 done = ready
         if not last:
             def send_rest(step, carry):
-                send_out(h, step + 1 - 2 * (step % 2))
+                send_out(h, (step // 2) * 2 + (step + h + 1) % 2)
                 return carry
 
             lax.fori_loop(0, columns, send_rest, 0)

time: 138 us -> 138 us (level)
  no operation moved by 1% of the time
where the time goes in v5:
time: 138 us; the launch traced here: 137 us
  Pallas kernels  135 us (98%)
    pallas_call x1, Pallas kernels, on_device(): pl.pallas_call(functools.partial(kernel, group_heads, seq_count, head_cou...  135 us

profile of v5, /device:TPU:3, one launch (start us, length us, event | category | flops | bytes accessed | tf_op | source)
XLA Modules:
  0.0 136.6 jit_solution(7800567564227545604)
XLA Ops:
  0.0 135.5 %shard_map.64 = bf16[144,5120]{1,0:T(8,128)(2,1)S(1)} custom-call(s32[5,1152]{1,0:T(8,128)} %bitcast.1, s32[3]{0:T(128)} %time_ref.1, s32[3]{0:T(128)} %width_ref.1, bf16[144,5120]{1,0:T(8,128)(2,1)} %q_ref.1, bf16[144,5120]{1,0:T(8,128)(2,1)} %k_ref.1, bf16[144,5120]{1,0:T(8,128)(2,1)} %v_ref.1), custom_call_target="tpu_custom_call" | custom-call | tf_op jit(solution)/shard_map/pallas_call | solution.py:287
  135.5 1.1 copy.8
